TPU v7x, 128 devices: a whole 4x4x4 slice. The times are simulated.
128 devices in a mesh: tiles: 128 (over x, z, y, core).
Axes of the slice: x: 4, y: 4, z: 4, core: 2. Of those that a mesh axis runs over, the one named last changes fastest.
Arguments:
- primal_start: float32 [256, 512, 1024], P('tiles'), may hold values from 0 to 1
- cost: bfloat16 [256, 512, 1024], P('tiles'), may hold values from -4 to 4
- mask: int32 [256, 64, 8], P('tiles'), may hold values 0 or 1
- tile_adv: int32 [256], P('tiles'), may hold values from -1 to 127, as said below
- tile_slot: int32 [256], P('tiles'), may hold values from -1 to 127
- adv_dual: float32 [128, 512], P('tiles'), may hold values from 0 to 2
- slot_dual: float32 [128, 1024], P('tiles'), may hold values from 0 to 2
- spend_limit: float32 [128, 512], P('tiles'), may hold values from 204 to 921
- capacity: float32 [128, 1024], P('tiles'), may hold values from 64 to 384
Outputs:
- primal: float32 [256, 512, 1024], P('tiles')
- adv_out: float32 [128, 512], P('tiles')
- slot_out: float32 [128, 1024], P('tiles')
Inputs may be any that keep to these rules, and one draw needn't show every extreme that they name: -1 marks an empty tile slot; tile_adv and tile_slot are -1 at the same slots. Each device's 2 slots hold 1 to 2 tiles, in its first slots, and some device holds exactly 2.
All inputs are finite; a program needn't handle non-finite values. No bound on the sum of `mask` on one device may be relied on, other than what follows from the above.
Results may differ from a plain program's by a relative error of at most 0.0003.
Values sent between devices are 32-bit elements; how exact they have to be, the bound alone decides.
No kernel may reach another device: no remote copies, remote signals or barrier semaphores. Data moves between devices by JAX's collectives and lax.ppermute only.
A program may use at most 64 MiB of HBM per device.

v0:
```python
import jax
import jax.numpy as jnp
from jax import lax
from jax.sharding import PartitionSpec as P

MB_ROWS = 8
MB_COLS = 128
ITERS = 2
tau_step = 0.5


def expand_mask(blocks, block_rows, block_cols):
    values = blocks.astype(jnp.float32)
    rows_in = values.shape[-2]
    cols_in = values.shape[-1]
    shaped = jnp.broadcast_to(
        values[..., :, None, :, None],
        values.shape[:-2] + (rows_in, block_rows, cols_in, block_cols),
    )
    return shaped.reshape(values.shape[:-2] + (rows_in * block_rows, cols_in * block_cols))


def body(primal_start, cost, mask, tile_adv, tile_slot, adv_dual, slot_dual, spend_limit, capacity):
    highest = lax.Precision.HIGHEST
    devices = lax.axis_size("tiles")
    adv_local = adv_dual.shape[0]
    slot_local = slot_dual.shape[0]
    rows_tile = primal_start.shape[1]
    cols_tile = primal_start.shape[2]
    adv_onehot = (
        tile_adv[:, None] == jnp.arange(adv_local * devices, dtype=jnp.int32)[None, :]
    ).astype(jnp.float32)
    slot_onehot = (
        tile_slot[:, None] == jnp.arange(slot_local * devices, dtype=jnp.int32)[None, :]
    ).astype(jnp.float32)
    present = (tile_adv >= 0).astype(jnp.float32)
    weight = expand_mask(mask, MB_ROWS, MB_COLS) * present[:, None, None]
    primal = weight * primal_start
    for sweep_index in range(ITERS):
        adv_all, slot_all = (
            lax.all_gather(adv_dual, "tiles", axis=0, tiled=True),
            lax.all_gather(slot_dual, "tiles", axis=0, tiled=True),
        )
        adv_rows = jnp.dot(adv_onehot, adv_all, precision=highest)
        slot_cols = jnp.dot(slot_onehot, slot_all, precision=highest)
        update = weight * jnp.clip(
            primal
            - tau_step * (cost.astype(jnp.float32) + adv_rows[:, :, None] + slot_cols[:, None, :]),
            0.0,
            1.0,
        )
        extended = 2.0 * update - primal
        row_blocks = jnp.dot(adv_onehot.T, jnp.sum(extended, axis=2), precision=highest)
        col_blocks = jnp.dot(slot_onehot.T, jnp.sum(extended, axis=1), precision=highest)
        primal, row_blocks, col_blocks = (update, row_blocks, col_blocks)
        row_mine, col_mine = (
            lax.psum_scatter(row_blocks, "tiles", scatter_dimension=0, tiled=True),
            lax.psum_scatter(col_blocks, "tiles", scatter_dimension=0, tiled=True),
        )
        adv_dual = jnp.maximum(adv_dual + (row_mine - spend_limit) / cols_tile, 0.0)
        slot_dual = jnp.maximum(slot_dual + (col_mine - capacity) / rows_tile, 0.0)
    return (primal, adv_dual, slot_dual)


def solution(mesh):
    return jax.shard_map(
        body,
        mesh=mesh,
        in_specs=(
            P("tiles", None, None),
            P("tiles", None, None),
            P("tiles", None, None),
            P("tiles"),
            P("tiles"),
            P("tiles", None),
            P("tiles", None),
            P("tiles", None),
            P("tiles", None),
        ),
        out_specs=(P("tiles", None, None), P("tiles", None), P("tiles", None)),
        check_vma=False,
    )
```

profile of v0, /device:TPU:1, one launch (start us, length us, event | category | flops | bytes accessed | tf_op | source)
XLA Modules:
  0.0 469.9 jit_solution(5772442257037595880)
XLA Ops:
  7.2 0.0 copy-start.3
  7.2 0.0 copy-start.4
  7.2 0.0 all-reduce.11.cloned.1.call-start
  7.2 0.7 compare_convert_fusion
  7.9 0.7 convert_element_type.12
  8.6 0.1 copy.13
  8.7 38.9 %all-gather = f32[128,1,512]{2,1,0:T(1,128)S(1)} all-gather(f32[1,1,512]{2,1,0:T(1,128)} %bitcast.50), channel_id=1, replica_groups=mesh['tiles'=128] {'tiles'}, dimensions={0}, use_global_device_ids=true | all-gather | bytes 264192 | tf_op jit(solution)/shard_map/all_gather | solution.py:41
  47.6 0.9 fusion.22
  48.4 33.9 %all-gather.1 = f32[128,1,1024]{2,1,0:T(1,128)S(1)} all-gather(f32[1,1,1024]{2,1,0:T(1,128)} %bitcast.49), channel_id=1, replica_groups=mesh['tiles'=128] {'tiles'}, dimensions={0}, use_global_device_ids=true | all-gather | bytes 528384 | tf_op jit(solution)/shard_map/all_gather | solution.py:42
  82.4 0.0 copy-start.5
  82.4 0.0 copy-start.6
  82.4 1.0 fusion.16
  83.4 0.0 copy-start.1
  83.4 0.0 copy-start.2
  83.4 0.0 copy-start
  83.4 5.0 %fusion.26 = (f32[2,512]{1,0:T(2,128)S(1)}, f32[2,1024]{1,0:T(2,128)S(1)}) fusion(f32[2,512,1024]{2,1,0:T(8,128)} %param.9, f32[2]{0:T(128)S(1)} %compare_convert_fusion, f32[2,64,8]{2,1,0:T(8,128)S(1)} %copy.13, f32[2,1024]{1,0:T(2,128)S(1)} %fusion.16, f32[2,512]{1,0:T(2,128)S(1)} %fusion.22, bf16[2,512,1024]{2,1,0:T(8,128)(2,1)} %param.10), kind=kLoop, calls=%fused_computation.31 | loop fusion | flops 13628416 | bytes 6320136 | tf_op jit(solution)/shard_map/reduce_sum | solution.py:53
  88.4 0.0 copy-done.3
  88.4 1.1 fusion.42
  89.5 0.0 copy-done.4
  89.5 1.3 fusion.40
  90.8 0.0 all-reduce.11.cloned.1.call-update
  90.8 0.0 all-reduce.9.cloned.1.call-start
  90.9 145.2 %all-reduce.11.cloned.1.call-done = (f32[128,1024]{1,0:T(8,128)}, f32[128,512]{1,0:T(8,128)}) async-done(((f32[128,1024]{1,0:T(8,128)}, f32[128,512]{1,0:T(8,128)}), (f32[128,1024]{1,0:T(8,128)}, f32[128,512]{1,0:T(8,128)})) %all-reduce.11.cloned.1.call-update) | async-done | bytes 786448
  236.0 0.0 copy-done.5
  236.0 0.0 copy-done.6
  236.0 0.7 fusion.37
  236.8 35.2 %all-gather.2 = f32[128,1,512]{2,1,0:T(1,128)S(1)} all-gather(f32[1,1,512]{2,1,0:T(1,128)S(1)} %bitcast.48), channel_id=1, replica_groups=mesh['tiles'=128] {'tiles'}, dimensions={0}, use_global_device_ids=true | all-gather | bytes 264192 | tf_op jit(solution)/shard_map/all_gather | solution.py:41
  272.0 0.2 fusion.19
  272.2 0.0 copy-done.1
  272.2 0.0 copy-done.2
  272.2 0.8 fusion.31
  273.0 34.0 %all-gather.3 = f32[128,1,1024]{2,1,0:T(1,128)S(1)} all-gather(f32[1,1,1024]{2,1,0:T(1,128)S(1)} %bitcast.47), channel_id=1, replica_groups=mesh['tiles'=128] {'tiles'}, dimensions={0}, use_global_device_ids=true | all-gather | bytes 528384 | tf_op jit(solution)/shard_map/all_gather | solution.py:42
  307.0 0.3 fusion.13
  307.3 0.0 copy-done
  307.3 6.4 %fusion.11 = (f32[2,1024]{1,0:T(2,128)S(1)}, f32[2,512]{1,0:T(2,128)S(1)}, f32[2,512,1024]{2,1,0:T(8,128)}) fusion(f32[2,1024]{1,0:T(2,128)S(1)} %fusion.16, f32[2,512]{1,0:T(2,128)S(1)} %fusion.22, bf16[2,512,1024]{2,1,0:T(8,128)(2,1)S(1)} %copy-done, f32[2,512,1024]{2,1,0:T(8,128)} %param.9, f32[2]{0:T(128)S(1)} %compare_convert_fusion, ...), kind=kLoop, calls=%fused_computation.16 | loop fusion | flops 19919872 | bytes 10526728 | tf_op jit(solution)/shard_map/reduce_sum | solution.py:54
  313.7 1.1 fusion.41
  314.8 1.3 fusion.39
  316.1 0.0 all-reduce.9.cloned.1.call-update
  316.1 144.2 %all-reduce.9.cloned.1.call-done = (f32[128,512]{1,0:T(8,128)}, f32[128,1024]{1,0:T(8,128)}) async-done(((f32[128,512]{1,0:T(8,128)}, f32[128,1024]{1,0:T(8,128)}), (f32[128,512]{1,0:T(8,128)}, f32[128,1024]{1,0:T(8,128)})) %all-reduce.9.cloned.1.call-update) | async-done | bytes 786448
  460.4 1.3 fusion.38
  461.7 1.4 fusion.32
Async XLA Ops:
  7.2 81.2 %copy-start.3 = (s32[2]{0:T(128)S(1)}, s32[2]{0:T(128)}, u32[]{:S(2)}) copy-start(s32[2]{0:T(128)} %param.12) | copy-start | bytes 28
  7.2 82.3 %copy-start.4 = (s32[2]{0:T(128)S(1)}, s32[2]{0:T(128)}, u32[]{:S(2)}) copy-start(s32[2]{0:T(128)} %param.13) | copy-start | bytes 28
  7.2 228.8 %all-reduce.11.cloned.1.call-start = ((), (), s32[]{:S(2)}) async-start(), calls=%async_computation.1 | async-start | bytes 1572864
  82.4 153.7 %copy-start.5 = (f32[1,512]{1,0:T(1,128)S(1)}, f32[1,512]{1,0:T(1,128)}, u32[]{:S(2)}) copy-start(f32[1,512]{1,0:T(1,128)} %param.14) | copy-start | bytes 6148
  82.4 153.7 %copy-start.6 = (f32[1,512]{1,0:T(1,128)S(1)}, f32[1,512]{1,0:T(1,128)}, u32[]{:S(2)}) copy-start(f32[1,512]{1,0:T(1,128)} %param.16) | copy-start | bytes 6148
  83.4 188.8 %copy-start.1 = (f32[1,1024]{1,0:T(1,128)S(1)}, f32[1,1024]{1,0:T(1,128)}, u32[]{:S(2)}) copy-start(f32[1,1024]{1,0:T(1,128)} %param.15) | copy-start | bytes 12292
  83.4 188.8 %copy-start.2 = (f32[1,1024]{1,0:T(1,128)S(1)}, f32[1,1024]{1,0:T(1,128)}, u32[]{:S(2)}) copy-start(f32[1,1024]{1,0:T(1,128)} %param.17) | copy-start | bytes 12292
  83.4 223.9 %copy-start = (bf16[2,512,1024]{2,1,0:T(8,128)(2,1)S(1)}, bf16[2,512,1024]{2,1,0:T(8,128)(2,1)}, u32[]{:S(2)}) copy-start(bf16[2,512,1024]{2,1,0:T(8,128)(2,1)} %param.10) | copy-start | bytes 6291460
  90.8 369.6 %all-reduce.9.cloned.1.call-start = ((), (), s32[]{:S(2)}) async-start(), calls=%async_computation | async-start | bytes 1572864
Sparse Core Ops, SparseCore 0:
  90.9 145.0 all-reduce.10
  316.2 144.0 all-reduce.8
where the time goes:
time: 471 us; the launch traced here: 470 us
  waiting for transfers between devices  289 us (61%)
  blocking collectives  142 us (30%)
  other arithmetic  16.9 us (4%)
  between operations  14.1 us (3%)
  matrix products  7.18 us (2%)
    unnamed x4, waiting for transfers between devices  289 us
    all_gather x2, blocking collectives, body(): lax.all_gather(adv_dual, 'tiles', axis=0, tiled=True)  74.1 us
    all_gather x2, blocking collectives, body(): lax.all_gather(slot_dual, 'tiles', axis=0, tiled=True)  67.9 us
  transfers between devices with their start and end apart: 2, of which 2 were waited for; matrix products, arithmetic and copies ran while one was open for 0% of the time, Pallas kernels for 0%

commit v1 on v0

--- a/solution.py
+++ b/solution.py
@@ -37,8 +37,20 @@
     weight = expand_mask(mask, MB_ROWS, MB_COLS) * present[:, None, None]
     primal = weight * primal_start
     for sweep_index in range(ITERS):
+
+        def _form_notes(x_part, join_dim):
+            return jnp.concatenate(
+                lax.all_to_all(
+                    jnp.stack([x_part] * lax.psum(1, axis_name="tiles")),
+                    axis_name="tiles",
+                    split_axis=0,
+                    concat_axis=0,
+                ),
+                axis=join_dim,
+            )
+
         adv_all, slot_all = (
-            lax.all_gather(adv_dual, "tiles", axis=0, tiled=True),
+            _form_notes(adv_dual, 0),
             lax.all_gather(slot_dual, "tiles", axis=0, tiled=True),
         )
         adv_rows = jnp.dot(adv_onehot, adv_all, precision=highest)

time: 471 us -> 425 us (0.902)
  blocking collectives: 142 us -> 75.4 us
  starting transfers between devices: 0.08 us -> 18.2 us
    all_gather x2 -> x0, blocking collectives: 74.1 us -> none  [body(): lax.all_gather(adv_dual, 'tiles', axis=0, tiled=True)]
    all_to_all x0 -> x2, starting transfers between devices: none -> 18.2 us  [_form_notes(): lax.all_to_all(jnp.stack([x_part] * lax.psum(1, axis_name='tiles')), axis...]
    all_gather x2, blocking collectives: 67.9 us -> 75.4 us  [body(): lax.all_gather(slot_dual, 'tiles', axis=0, tiled=True)]
  transfers between devices with their start and end apart: 2 -> 4, of which waited for: 2 -> 2; matrix products, arithmetic and copies ran while one was open for 0% -> 1% of each run, Pallas kernels for 0% -> 0%
where the time goes in v1:
time: 425 us; the launch traced here: 424 us
  waiting for transfers between devices  290 us (68%)
  blocking collectives  75.4 us (18%)
  starting transfers between devices  18.2 us (4%)
  other arithmetic  16.9 us (4%)
  between operations  14.1 us (3%)
  matrix products  7.15 us (2%)
    unnamed x4, waiting for transfers between devices  290 us
    all_gather x2, blocking collectives, body(): lax.all_gather(slot_dual, 'tiles', axis=0, tiled=True)  75.4 us
    all_to_all x2, starting transfers between devices, _form_notes(): lax.all_to_all(jnp.stack([x_part] * lax.psum(1, axis_name='tiles')), axis...  18.2 us
  transfers between devices with their start and end apart: 4, of which 2 were waited for; matrix products, arithmetic and copies ran while one was open for 1% of the time, Pallas kernels for 0%

profile of v1, /device:TPU:1, one launch (start us, length us, event | category | flops | bytes accessed | tf_op | source)
XLA Modules:
  0.0 424.1 jit_solution(9012968819520928089)
XLA Ops:
  7.2 1.5 stack.4
  8.7 0.0 copy-start.3
  8.7 0.0 copy-start.4
  8.7 11.5 %all-to-all-start = ((f32[128,1,512]{2,1,0:T(1,128)}), f32[128,1,512]{2,1,0:T(1,128)S(1)}, u32[]{:S(2)}, u32[]{:S(2)}) async-start(f32[128,1,512]{2,1,0:T(1,128)} %stack.4), calls=%async_computation | async-start | bytes 524288 | tf_op jit(solution)/shard_map/all_to_all | solution.py:43
  20.2 0.0 all-reduce.11.cloned.1.call-start
  20.2 37.7 %all-gather = f32[128,1,1024]{2,1,0:T(1,128)S(1)} all-gather(f32[1,1,1024]{2,1,0:T(1,128)} %bitcast.49), channel_id=1, replica_groups=mesh['tiles'=128] {'tiles'}, dimensions={0}, use_global_device_ids=true | all-gather | bytes 528384 | tf_op jit(solution)/shard_map/all_gather | solution.py:54
  57.9 0.7 compare_convert_fusion
  58.6 0.7 convert_element_type.12
  59.3 0.1 copy.13
  59.4 1.0 fusion.16
  60.4 0.0 copy-start.5
  60.4 0.0 copy-start.6
  60.4 0.0 all-to-all-done
  60.4 0.9 fusion.22
  61.3 0.0 copy-start.1
  61.3 0.0 copy-start.2
  61.3 0.0 copy-start
  61.3 5.0 %fusion.26 = (f32[2,512]{1,0:T(2,128)S(1)}, f32[2,1024]{1,0:T(2,128)S(1)}) fusion(f32[2,512,1024]{2,1,0:T(8,128)} %param.9, f32[2]{0:T(128)S(1)} %compare_convert_fusion, f32[2,64,8]{2,1,0:T(8,128)S(1)} %copy.13, f32[2,1024]{1,0:T(2,128)S(1)} %fusion.16, f32[2,512]{1,0:T(2,128)S(1)} %fusion.22, bf16[2,512,1024]{2,1,0:T(8,128)(2,1)} %param.10), kind=kLoop, calls=%fused_computation.31 | loop fusion | flops 13628416 | bytes 6320136 | tf_op jit(solution)/shard_map/reduce_sum | solution.py:65
  66.3 0.0 copy-done.3
  66.3 1.1 fusion.42
  67.4 0.0 copy-done.4
  67.4 1.3 fusion.40
  68.7 0.0 all-reduce.11.cloned.1.call-update
  68.7 144.9 %all-reduce.11.cloned.1.call-done = (f32[128,1024]{1,0:T(8,128)}, f32[128,512]{1,0:T(8,128)}) async-done(((f32[128,1024]{1,0:T(8,128)}, f32[128,512]{1,0:T(8,128)}), (f32[128,1024]{1,0:T(8,128)}, f32[128,512]{1,0:T(8,128)})) %all-reduce.11.cloned.1.call-update) | async-done | bytes 786448
  213.6 0.0 copy-done.5
  213.6 0.0 copy-done.6
  213.6 0.7 fusion.37
  214.4 0.8 stack.5
  215.2 6.7 %all-to-all-start.1 = ((f32[128,1,512]{2,1,0:T(1,128)}), f32[128,1,512]{2,1,0:T(1,128)S(1)}, u32[]{:S(2)}, u32[]{:S(2)}) async-start(f32[128,1,512]{2,1,0:T(1,128)} %stack.5), calls=%async_computation.1 | async-start | bytes 524288 | tf_op jit(solution)/shard_map/all_to_all | solution.py:43
  221.9 0.0 all-reduce.9.cloned.1.call-start
  221.9 0.0 copy-done.1
  221.9 0.0 copy-done.2
  221.9 0.8 fusion.31
  222.7 37.7 %all-gather.1 = f32[128,1,1024]{2,1,0:T(1,128)S(1)} all-gather(f32[1,1,1024]{2,1,0:T(1,128)S(1)} %bitcast.47), channel_id=1, replica_groups=mesh['tiles'=128] {'tiles'}, dimensions={0}, use_global_device_ids=true | all-gather | bytes 528384 | tf_op jit(solution)/shard_map/all_gather | solution.py:54
  260.4 0.3 fusion.13
  260.7 0.0 all-to-all-done.1
  260.8 0.2 fusion.19
  261.0 0.0 copy-done
  261.0 6.4 %fusion.11 = (f32[2,1024]{1,0:T(2,128)S(1)}, f32[2,512]{1,0:T(2,128)S(1)}, f32[2,512,1024]{2,1,0:T(8,128)}) fusion(f32[2,1024]{1,0:T(2,128)S(1)} %fusion.16, f32[2,512]{1,0:T(2,128)S(1)} %fusion.22, bf16[2,512,1024]{2,1,0:T(8,128)(2,1)S(1)} %copy-done, f32[2,512,1024]{2,1,0:T(8,128)} %param.9, f32[2]{0:T(128)S(1)} %compare_convert_fusion, ...), kind=kLoop, calls=%fused_computation.16 | loop fusion | flops 19919872 | bytes 10526728 | tf_op jit(solution)/shard_map/reduce_sum | solution.py:66
  267.4 1.1 fusion.41
  268.5 1.3 fusion.39
  269.7 0.0 all-reduce.9.cloned.1.call-update
  269.8 144.9 %all-reduce.9.cloned.1.call-done = (f32[128,512]{1,0:T(8,128)}, f32[128,1024]{1,0:T(8,128)}) async-done(((f32[128,512]{1,0:T(8,128)}, f32[128,1024]{1,0:T(8,128)}), (f32[128,512]{1,0:T(8,128)}, f32[128,1024]{1,0:T(8,128)})) %all-reduce.9.cloned.1.call-update) | async-done | bytes 786448
  414.6 1.3 fusion.38
  415.9 1.4 fusion.32
Async XLA Ops:
  8.7 57.6 %copy-start.3 = (s32[2]{0:T(128)S(1)}, s32[2]{0:T(128)}, u32[]{:S(2)}) copy-start(s32[2]{0:T(128)} %param.12) | copy-start | bytes 28
  8.7 58.7 %copy-start.4 = (s32[2]{0:T(128)S(1)}, s32[2]{0:T(128)}, u32[]{:S(2)}) copy-start(s32[2]{0:T(128)} %param.13) | copy-start | bytes 28
  8.7 51.7 %all-to-all-start = ((f32[128,1,512]{2,1,0:T(1,128)}), f32[128,1,512]{2,1,0:T(1,128)S(1)}, u32[]{:S(2)}, u32[]{:S(2)}) async-start(f32[128,1,512]{2,1,0:T(1,128)} %stack.4), calls=%async_computation | async-start | bytes 524288 | tf_op jit(solution)/shard_map/all_to_all | solution.py:43
  20.2 193.4 %all-reduce.11.cloned.1.call-start = ((), (), s32[]{:S(2)}) async-start(), calls=%async_computation.3 | async-start | bytes 1572864
  60.4 153.3 %copy-start.5 = (f32[1,512]{1,0:T(1,128)S(1)}, f32[1,512]{1,0:T(1,128)}, u32[]{:S(2)}) copy-start(f32[1,512]{1,0:T(1,128)} %param.14) | copy-start | bytes 6148
  60.4 153.2 %copy-start.6 = (f32[1,512]{1,0:T(1,128)S(1)}, f32[1,512]{1,0:T(1,128)}, u32[]{:S(2)}) copy-start(f32[1,512]{1,0:T(1,128)} %param.16) | copy-start | bytes 6148
  61.3 160.7 %copy-start.1 = (f32[1,1024]{1,0:T(1,128)S(1)}, f32[1,1024]{1,0:T(1,128)}, u32[]{:S(2)}) copy-start(f32[1,1024]{1,0:T(1,128)} %param.15) | copy-start | bytes 12292
  61.3 160.7 %copy-start.2 = (f32[1,1024]{1,0:T(1,128)S(1)}, f32[1,1024]{1,0:T(1,128)}, u32[]{:S(2)}) copy-start(f32[1,1024]{1,0:T(1,128)} %param.17) | copy-start | bytes 12292
  61.3 199.7 %copy-start = (bf16[2,512,1024]{2,1,0:T(8,128)(2,1)S(1)}, bf16[2,512,1024]{2,1,0:T(8,128)(2,1)}, u32[]{:S(2)}) copy-start(bf16[2,512,1024]{2,1,0:T(8,128)(2,1)} %param.10) | copy-start | bytes 6291460
  215.2 45.6 %all-to-all-start.1 = ((f32[128,1,512]{2,1,0:T(1,128)}), f32[128,1,512]{2,1,0:T(1,128)S(1)}, u32[]{:S(2)}, u32[]{:S(2)}) async-start(f32[128,1,512]{2,1,0:T(1,128)} %stack.5), calls=%async_computation.1 | async-start | bytes 524288 | tf_op jit(solution)/shard_map/all_to_all | solution.py:43
  221.9 192.8 %all-reduce.9.cloned.1.call-start = ((), (), s32[]{:S(2)}) async-start(), calls=%async_computation.2 | async-start | bytes 1572864
Sparse Core Ops, SparseCore 0:
  68.8 144.7 all-reduce.10
  269.9 144.7 all-reduce.8
